TPU v7x, 32 devices: a whole 2x2x4 slice. The times are simulated.
32 devices in a mesh: groups: 2 (over y), tm: 4 (over z), rows: 4 (over x, core).
Axes of the slice: x: 2, y: 2, z: 4, core: 2. Of those that a mesh axis runs over, the one named last changes fastest.
Arguments:
- latents: bfloat16 [16, 16, 128, 256], P(('groups', 'tm'), 'rows'), parts along dimension 0, may hold values from -6 to 6
- weight_in: bfloat16 [3, 3, 256, 256], replicated, may hold values from -0.125 to 0.125
- weight_out: bfloat16 [3, 3, 256, 256], replicated, may hold values from -0.0234375 to 0.0234375
- decay_table: float32 [16], replicated, may hold values from 0.99 to 0.999
- decay_index: int32 [256], replicated, may hold values from 0 to 15
Outputs:
- updated: bfloat16 [16, 16, 128, 256], P(('groups', 'tm'), 'rows'), parts along dimension 0
There are 2 independent parts, one for each index of `groups`. A program takes and returns all parts, laid end to end along the dimension named above; an argument that names none is the same for every part. Nothing has to cross between parts.
All inputs are finite; a program needn't handle non-finite values.
Results may differ from a plain program's by a relative error of at most 0.0032.
Values may be sent and summed in bfloat16 or wider, within the bound.
A program may use at most 64 MiB of HBM per device.

v0:
```python
import functools

import jax
import jax.numpy as jnp
from jax import lax
from jax.experimental import pallas as pl
from jax.experimental.pallas import tpu as pltpu
from jax.sharding import PartitionSpec as P

MESH = pl.DeviceIdType.MESH
PIECES = 4


def kernel(
    positions,
    strips,
    lat_hbm,
    win_hbm,
    wout_hbm,
    table_hbm,
    index_hbm,
    out_hbm,
    lat,
    win,
    wout,
    halo,
    wide,
    partial,
    carry,
    passed,
    rounded,
    state_halo,
    relayed,
    mixed,
    table_ref,
    index_ref,
    wide_states,
    result,
    load_sem,
    store_sem,
    halo_send,
    halo_recv,
    state_send,
    state_recv,
    carry_send,
    carry_recv,
    relay_send,
    relay_recv,
):
    frames, strip, width, channels = lat.shape
    row = lax.axis_index("rows")
    moment = lax.axis_index("tm")
    has_up, has_down = row > 0, row < strips - 1
    has_before, has_after = moment > 0, moment < positions - 1
    span = width // PIECES

    load_lat = pltpu.make_async_copy(lat_hbm, lat, load_sem.at[0])
    load_win = pltpu.make_async_copy(win_hbm, win, load_sem.at[1])
    load_wout = pltpu.make_async_copy(wout_hbm, wout, load_sem.at[2])
    load_table = pltpu.make_async_copy(table_hbm, table_ref, load_sem.at[3])
    load_index = pltpu.make_async_copy(index_hbm, index_ref, load_sem.at[4])

    barrier = pltpu.get_barrier_semaphore()
    near = (
        (has_up, {"rows": row - 1}),
        (has_down, {"rows": row + 1}),
        (has_before, {"tm": moment - 1}),
        (has_after, {"tm": moment + 1}),
    )
    total = 0
    for exists, where in near:
        total = total + exists.astype(jnp.int32)

        @pl.when(exists)
        def _():
            pl.semaphore_signal(barrier, inc=1, device_id=where, device_id_type=MESH)

    load_lat.start()
    load_table.start()
    load_index.start()
    load_win.start()
    load_wout.start()
    pl.semaphore_wait(barrier, total)

    def halo_copy(side):
        source = lat_hbm.at[:, strip - 1] if side == 0 else lat_hbm.at[:, 0]
        target = row + 1 if side == 0 else row - 1
        return pltpu.make_async_remote_copy(
            src_ref=source,
            dst_ref=halo.at[side],
            send_sem=halo_send.at[side],
            recv_sem=halo_recv.at[side],
            device_id={"rows": target},
            device_id_type=MESH,
        )

    def state_copy(side):
        source = rounded.at[strip - 1] if side == 0 else rounded.at[0]
        target = row + 1 if side == 0 else row - 1
        return pltpu.make_async_remote_copy(
            src_ref=source,
            dst_ref=state_halo.at[side],
            send_sem=state_send.at[side],
            recv_sem=state_recv.at[side],
            device_id={"rows": target},
            device_id_type=MESH,
        )

    def relay_copy(side, piece):
        part = pl.ds(piece * span, span)
        edge = strip - 1 if side == 0 else 0
        target = row + 1 if side == 0 else row - 1
        return pltpu.make_async_remote_copy(
            src_ref=carry.at[edge, part],
            dst_ref=relayed.at[side, part],
            send_sem=relay_send.at[side, piece],
            recv_sem=relay_recv.at[side, piece],
            device_id={"rows": target},
            device_id_type=MESH,
        )

    def carry_copy(i, piece):
        part = pl.ds(piece * span, span)
        return pltpu.make_async_remote_copy(
            src_ref=passed.at[i, part],
            dst_ref=carry.at[i, part],
            send_sem=carry_send.at[i, piece],
            recv_sem=carry_recv.at[i, piece],
            device_id={"tm": moment + 1},
            device_id_type=MESH,
        )

    even = lax.rem(row, 2) == 0

    @pl.when(jnp.logical_and(has_up, even))
    def _():
        halo_copy(1).start()

    @pl.when(has_down)
    def _():
        halo_copy(0).start()

    @pl.when(jnp.logical_and(has_up, jnp.logical_not(even)))
    def _():
        halo_copy(1).start()

    load_table.wait()
    load_index.wait()
    chosen = index_ref[...]
    decays = jnp.zeros(chosen.shape, jnp.float32)
    for level in range(table_ref.shape[0]):
        decays = jnp.where(chosen == level, table_ref[level], decays)
    growth = [decays]
    for _ in range(frames - 1):
        growth.append(growth[-1] * decays)

    column = lax.broadcasted_iota(jnp.int32, (width, channels), 0)

    def spread(target, place, frame, value):
        full = value.astype(jnp.float32)
        before = jnp.where(column == 0, 0.0, pltpu.roll(full, 1, 0))
        after = jnp.where(column == width - 1, 0.0, pltpu.roll(full, width - 1, 0))
        target[place, frame, :, 0:channels] = before.astype(jnp.bfloat16)
        target[place, frame, :, channels : 2 * channels] = value
        target[place, frame, :, 2 * channels : 3 * channels] = after.astype(jnp.bfloat16)

    def border(i, side, exists):
        @pl.when(exists)
        def _():
            halo_copy(side).wait_recv()
            for frame in range(frames):
                spread(wide, i, frame, halo[side, frame])

        @pl.when(jnp.logical_not(exists))
        def _():
            wide[i] = jnp.zeros(wide.shape[1:], wide.dtype)

    def drive(i):
        window = jnp.concatenate([wide[i], wide[i + 1], wide[i + 2]], axis=-1)
        flat = window.reshape(frames * width, 9 * channels)
        driven = jnp.dot(flat, win[...], preferred_element_type=jnp.float32).reshape(
            frames, width, channels
        )
        running = driven[0]
        partial[i, 0] = running
        for frame in range(1, frames):
            running = decays * running + driven[frame]
            partial[i, frame] = running

    def begin(i):
        @pl.when(jnp.logical_not(has_before))
        def _():
            passed[i] = partial[i, frames - 1].astype(passed.dtype)

            @pl.when(has_after)
            def _():
                for piece in range(PIECES):
                    carry_copy(i, piece).start()

    def settle(i, side, exists):
        begin(i)
        for frame in range(frames):
            rounded[i, frame] = partial[i, frame].astype(jnp.bfloat16)

        @pl.when(exists)
        def _():
            state_copy(side).start()

    def advance(i, side=None, exists=None):
        for piece in range(PIECES):
            part = pl.ds(piece * span, span)
            carry_copy(i, piece).wait_recv()
            if side is not None:

                @pl.when(exists)
                def _():
                    relay_copy(side, piece).start()

            arrived = carry[i, part].astype(jnp.float32)
            last = partial[i, frames - 1, part] + growth[frames - 1] * arrived
            passed[i, part] = last.astype(passed.dtype)

            @pl.when(has_after)
            def _():
                carry_copy(i, piece).start()

            partial[i, frames - 1, part] = last
            for frame in range(frames - 1):
                partial[i, frame, part] = partial[i, frame, part] + growth[frame] * arrived

    def stretch(i):
        for frame in range(frames):
            spread(wide_states, i + 1, frame, partial[i, frame].astype(jnp.bfloat16))

    def outer(place, side, exists):
        @pl.when(exists)
        def _():
            state_copy(side).wait_recv()

            @pl.when(has_before)
            def _():
                for piece in range(PIECES):
                    relay_copy(side, piece).wait_recv()
                arrived = relayed[side].astype(jnp.float32)
                for frame in range(frames):
                    state = state_halo[side, frame].astype(jnp.float32)
                    state = state + growth[frame] * arrived
                    spread(wide_states, place, frame, state.astype(jnp.bfloat16))

            @pl.when(jnp.logical_not(has_before))
            def _():
                for frame in range(frames):
                    spread(wide_states, place, frame, state_halo[side, frame])

    def product(i, taps):
        window = [wide_states[i + tap] for tap in taps]
        window = window[0] if len(taps) == 1 else jnp.concatenate(window, axis=-1)
        flat = window.reshape(frames * width, len(taps) * 3 * channels)
        depth = 3 * channels
        rows = [wout[tap * depth : (tap + 1) * depth] for tap in taps]
        rows = rows[0] if len(taps) == 1 else jnp.concatenate(rows, axis=0)
        value = jnp.dot(flat, rows, preferred_element_type=jnp.float32)
        return value.reshape(frames, width, channels)

    def write(i, value):
        for frame in range(frames):
            updated = lat[frame, i].astype(jnp.float32) + jax.nn.gelu(value[frame])
            result[frame, i] = updated.astype(jnp.bfloat16)
        pltpu.make_async_copy(result.at[:, i], out_hbm.at[:, i], store_sem.at[i]).start()

    def close(side, exists):
        i, place, low = (0, 0, 0) if side == 0 else (strip - 1, strip + 1, 2)
        outer(place, side, exists)

        @pl.when(exists)
        def _():
            write(i, mixed[i] + product(i, [low]))

        @pl.when(jnp.logical_not(exists))
        def _():
            write(i, mixed[i])

    middle = list(range(1, strip - 1))
    bottom = strip - 1

    load_lat.wait()
    for i in range(strip):
        for frame in range(frames):
            spread(wide, i + 1, frame, lat[frame, i])
    load_win.wait()

    def drive_top():
        border(0, 0, has_up)
        drive(0)
        settle(0, 1, has_up)

    def drive_bottom():
        border(strip + 1, 1, has_down)
        drive(bottom)
        settle(bottom, 0, has_down)

    def by_parity(one, two):
        @pl.when(even)
        def _():
            one()

        @pl.when(jnp.logical_not(even))
        def _():
            two()

    late = middle[1:]
    early = moment == 1

    for i in middle[:1]:
        drive(i)
        begin(i)
    by_parity(drive_bottom, drive_top)
    for i in late:
        drive(i)

    @pl.when(early)
    def _():
        for i in middle[:1]:
            advance(i)

    by_parity(drive_top, drive_bottom)
    for i in late:
        begin(i)

    @pl.when(jnp.logical_and(has_before, jnp.logical_not(early)))
    def _():
        for i in middle[:1]:
            advance(i)

    @pl.when(has_before)
    def _():
        def low_first():
            advance(bottom, 0, has_down)
            advance(0, 1, has_up)

        def high_first():
            advance(0, 1, has_up)
            advance(bottom, 0, has_down)

        by_parity(low_first, high_first)

    @pl.when(jnp.logical_and(has_before, has_after))
    def _():
        for i in late:
            advance(i)

    load_wout.wait()
    ready = [i for i in range(strip) if i not in late]
    for i in ready:
        stretch(i)
    for i in range(strip):
        taps = [tap for tap in range(3) if i + tap - 1 in ready]
        mixed[i] = product(i, taps) if taps else jnp.zeros(mixed.shape[1:], jnp.float32)

    @pl.when(jnp.logical_and(has_before, jnp.logical_not(has_after)))
    def _():
        for i in late:
            advance(i)

    for i in late:
        stretch(i)
    for i in range(strip):
        taps = [tap for tap in range(3) if i + tap - 1 in late]
        if i in middle:
            write(i, mixed[i] + product(i, taps) if taps else mixed[i])
        elif taps:
            mixed[i] = mixed[i] + product(i, taps)

    def top_last():
        close(1, has_down)
        close(0, has_up)

    def bottom_last():
        close(0, has_up)
        close(1, has_down)

    by_parity(top_last, bottom_last)

    @pl.when(has_down)
    def _():
        halo_copy(0).wait_send()
        state_copy(0).wait_send()

    @pl.when(has_up)
    def _():
        halo_copy(1).wait_send()
        state_copy(1).wait_send()

    @pl.when(jnp.logical_and(has_down, has_before))
    def _():
        for piece in range(PIECES):
            relay_copy(0, piece).wait_send()

    @pl.when(jnp.logical_and(has_up, has_before))
    def _():
        for piece in range(PIECES):
            relay_copy(1, piece).wait_send()

    @pl.when(has_after)
    def _():
        for i in range(strip):
            for piece in range(PIECES):
                carry_copy(i, piece).wait_send()

    for i in range(strip):
        pltpu.make_async_copy(result.at[:, i], out_hbm.at[:, i], store_sem.at[i]).wait()


def local(positions, strips, latents, weight_in, weight_out, decay_table, decay_index):
    frames, strip, width, channels = latents.shape
    link = jnp.bfloat16 if positions <= 8 else jnp.float32
    half = jnp.bfloat16
    dma = pltpu.SemaphoreType.DMA
    anywhere = pl.BlockSpec(memory_space=pl.ANY)
    return pl.pallas_call(
        functools.partial(kernel, positions, strips),
        out_shape=jax.ShapeDtypeStruct(latents.shape, latents.dtype),
        in_specs=[
            anywhere,
            anywhere,
            anywhere,
            anywhere,
            anywhere,
        ],
        out_specs=anywhere,
        scratch_shapes=[
            pltpu.VMEM((frames, strip, width, channels), half),
            pltpu.VMEM((9 * channels, channels), half),
            pltpu.VMEM((9 * channels, channels), half),
            pltpu.VMEM((2, frames, width, channels), half),
            pltpu.VMEM((strip + 2, frames, width, 3 * channels), half),
            pltpu.VMEM((strip, frames, width, channels), jnp.float32),
            pltpu.VMEM((strip, width, channels), link),
            pltpu.VMEM((strip, width, channels), link),
            pltpu.VMEM((strip, frames, width, channels), half),
            pltpu.VMEM((2, frames, width, channels), half),
            pltpu.VMEM((2, width, channels), link),
            pltpu.VMEM((strip, frames, width, channels), jnp.float32),
            pltpu.SMEM(decay_table.shape, jnp.float32),
            pltpu.VMEM((1, channels), jnp.int32),
            pltpu.VMEM((strip + 2, frames, width, 3 * channels), half),
            pltpu.VMEM((frames, strip, width, channels), half),
            dma((5,)),
            dma((strip,)),
            dma((2,)),
            dma((2,)),
            dma((2,)),
            dma((2,)),
            dma((strip, PIECES)),
            dma((strip, PIECES)),
            dma((2, PIECES)),
            dma((2, PIECES)),
        ],
        compiler_params=pltpu.CompilerParams(collective_id=0, has_side_effects=True, vmem_limit_bytes=32 * 1024 * 1024),
    )(
        pltpu.with_memory_space_constraint(latents, pltpu.HBM),
        pltpu.with_memory_space_constraint(weight_in.reshape(9 * channels, channels), pltpu.HBM),
        pltpu.with_memory_space_constraint(weight_out.reshape(9 * channels, channels), pltpu.HBM),
        pltpu.with_memory_space_constraint(decay_table, pltpu.HBM),
        pltpu.with_memory_space_constraint(decay_index.reshape(1, channels), pltpu.HBM),
    )


def solution(mesh):
    in_specs = (P(("groups", "tm"), "rows", None, None), P(), P(), P(), P())
    out_specs = P(("groups", "tm"), "rows", None, None)
    body = functools.partial(local, mesh.shape["tm"], mesh.shape["rows"])
    return jax.shard_map(body, mesh=mesh, in_specs=in_specs, out_specs=out_specs, check_vma=False)
```

profile of v0, /device:TPU:29, one launch (start us, length us, event | category | flops | bytes accessed | tf_op | source)
XLA Modules:
  0.0 18.1 jit_solution(9766474896613346357)
XLA Ops:
  0.0 17.3 %shard_map.55 = bf16[2,4,128,256]{3,2,1,0:T(8,128)(2,1)S(1)} custom-call(bf16[2,4,128,256]{3,2,1,0:T(8,128)(2,1)} %lat_hbm.1, bf16[2304,256]{1,0:T(8,128)(2,1)} %bitcast.3, bf16[2304,256]{1,0:T(8,128)(2,1)} %bitcast.4, f32[16]{0:T(128)} %table_hbm.1, s32[1,256]{1,0:T(1,128)} %bitcast.5), custom_call_target="tpu_custom_call" | custom-call | tf_op jit(solution)/shard_map/pallas_call | solution.py:420
  17.3 0.8 %copy.7 = bf16[2,4,128,256]{3,2,1,0:T(8,128)(2,1)} copy(bf16[2,4,128,256]{3,2,1,0:T(8,128)(2,1)S(1)} %shard_map.55) | data formatting | bytes 1048576
where the time goes:
time: 18.3 us; the launch traced here: 18.1 us
  Pallas kernels  17.3 us (95%)
  local copies, waits for them, and re-layouts  0.8 us (4%)
    pallas_call x1, Pallas kernels, local(): pl.pallas_call(functools.partial(kernel, positions, strips), out_shape=ja...  17.3 us
    unnamed x1, local copies, waits for them, and re-layouts  0.8 us

commit v1 on v0

v1 whole, which is shorter than its diff:
```python
import functools

import jax
import jax.numpy as jnp
from jax import lax
from jax.experimental import pallas as pl
from jax.experimental.pallas import tpu as pltpu
from jax.sharding import PartitionSpec as P

MESH = pl.DeviceIdType.MESH
PIECES = 4


def kernel(
    positions,
    strips,
    lat_hbm,
    win_hbm,
    wout_hbm,
    table_hbm,
    index_hbm,
    out_hbm,
    lat,
    win,
    wout,
    wide,
    partial,
    share,
    shared,
    carry,
    passed,
    relayed,
    mixed,
    table_ref,
    index_ref,
    wide_states,
    result,
    lat_sem,
    win_sem,
    wout_sem,
    small_sem,
    store_sem,
    share_send,
    share_recv,
    carry_send,
    carry_recv,
    relay_send,
    relay_recv,
    turn,
):
    frames, strip, width, channels = lat.shape
    row = lax.axis_index("rows")
    moment = lax.axis_index("tm")
    odd = lax.rem(row, 2)
    span = width // PIECES
    bottom = strip - 1
    final = frames - 1
    edge = (0, bottom)
    ghost = (strip, strip + 1)
    near = (row - 1 + 2 * odd, row + 1 - 2 * odd)
    has = tuple(jnp.logical_and(at >= 0, at < strips) for at in near)
    paired = strips % 2 == 0
    depth = 3 * channels
    has_before, has_after = moment > 0, moment < positions - 1

    def guard(side):
        if side == 1 and paired:
            return lambda act: act()
        return pl.when(has[side])

    def place(i, count):
        return i + odd * (count - 1 - 2 * i)

    barrier = pltpu.get_barrier_semaphore()
    greeted = (
        (has[0], {"rows": near[0]}),
        (has[1], {"rows": near[1]}),
        (has_before, {"tm": moment - 1}),
        (has_after, {"tm": moment + 1}),
    )
    total = 0
    for exists, where in greeted:
        total = total + exists.astype(jnp.int32)

        @pl.when(exists)
        def _():
            pl.semaphore_signal(barrier, inc=1, device_id=where, device_id_type=MESH)

    def load_lat(i):
        return pltpu.make_async_copy(lat_hbm.at[:, place(i, strip)], lat.at[:, i], lat_sem.at[i])

    def load_win(tap):
        return pltpu.make_async_copy(win_hbm.at[place(tap, 3)], win.at[pl.ds(tap * depth, depth)], win_sem.at[tap])

    def load_wout(tap):
        return pltpu.make_async_copy(wout_hbm.at[place(tap, 3)], wout.at[pl.ds(tap * depth, depth)], wout_sem.at[tap])

    load_table = pltpu.make_async_copy(table_hbm, table_ref, small_sem.at[0])
    load_index = pltpu.make_async_copy(index_hbm, index_ref, small_sem.at[1])

    load_table.start()
    load_index.start()
    for i in range(strip):
        load_lat(i).start()
    for tap in range(3):
        load_win(tap).start()

    def share_copy(side, kind, frame):
        return pltpu.make_async_remote_copy(
            src_ref=share.at[side, kind, frame],
            dst_ref=shared.at[side, kind, frame],
            send_sem=share_send.at[side, kind, frame],
            recv_sem=share_recv.at[side, kind, frame],
            device_id={"rows": near[side]},
            device_id_type=MESH,
        )

    def relay_copy():
        return pltpu.make_async_remote_copy(
            src_ref=carry.at[bottom],
            dst_ref=relayed,
            send_sem=relay_send,
            recv_sem=relay_recv,
            device_id={"rows": near[1]},
            device_id_type=MESH,
        )

    def carry_copy(i, piece):
        part = pl.ds(piece * span, span)
        return pltpu.make_async_remote_copy(
            src_ref=passed.at[i, part],
            dst_ref=carry.at[i, part],
            send_sem=carry_send.at[i, piece],
            recv_sem=carry_recv.at[i, piece],
            device_id={"tm": moment + 1},
            device_id_type=MESH,
        )

    column = lax.broadcasted_iota(jnp.int32, (width, channels), 0)

    def spread(value):
        full = value.astype(jnp.float32)
        before = jnp.where(column == 0, 0.0, pltpu.roll(full, 1, 0))
        after = jnp.where(column == width - 1, 0.0, pltpu.roll(full, width - 1, 0))
        middle = value.astype(jnp.bfloat16)
        return jnp.concatenate([before.astype(jnp.bfloat16), middle, after.astype(jnp.bfloat16)], axis=-1)

    def prepare(i):
        load_lat(i).wait()
        for frame in range(frames):
            wide[i, frame] = spread(lat[frame, i])

    def times(rows, weights, taps):
        window = [r.reshape(frames * width, 3 * channels) for r in rows]
        window = window[0] if len(rows) == 1 else jnp.concatenate(window, axis=-1)
        factor = weights[taps[0] * depth : (taps[-1] + 1) * depth]
        value = jnp.dot(window, factor, preferred_element_type=jnp.float32)
        return value.reshape(frames, width, channels)

    def scan(value):
        running = [value[0]]
        for frame in range(1, frames):
            running.append(decays * running[-1] + value[frame])
        return running

    def drive(i):
        taps = [tap for tap in range(3) if 0 <= i + tap - 1 < strip]
        states = scan(times([wide[i + tap - 1] for tap in taps], win, taps))
        for frame in range(frames):
            partial[i, frame] = states[frame]
            if i in edge:
                share[edge.index(i), 1, frame] = states[frame].astype(jnp.bfloat16)

    def offer(side):
        states = scan(times([wide[edge[side]]], win, [2 - 2 * side]))
        for frame in range(frames):
            partial[ghost[side], frame] = states[frame]
            share[side, 0, frame] = states[frame].astype(jnp.bfloat16)

    def send(side):
        @guard(side)
        def _():
            for frame in reversed(range(frames)):
                for kind in range(2):
                    share_copy(side, kind, frame).start()

    def absorb(side, which, kinds=(0, 1)):
        for frame in which:
            for kind in kinds:
                share_copy(side, kind, frame).wait_recv()
                i = (edge, ghost)[kind][side]
                partial[i, frame] = partial[i, frame] + shared[side, kind, frame].astype(jnp.float32)

    def block(act):
        pl.when(row >= 0)(act)

    def begin(i, pieces=range(PIECES)):
        for piece in pieces:
            part = pl.ds(piece * span, span)
            passed[i, part] = partial[i, final, part].astype(passed.dtype)
            carry_copy(i, piece).start()

    def advance(i, piece, last):
        part = pl.ds(piece * span, span)
        carry_copy(i, piece).wait_recv()
        if not last:
            value = partial[i, final, part] + growth[final] * carry[i, part].astype(jnp.float32)
            passed[i, part] = value.astype(passed.dtype)
            carry_copy(i, piece).start()

    def sent(i, pieces=range(PIECES)):
        for piece in pieces:
            carry_copy(i, piece).wait_send()

    def stretch(i, carried):
        if carried:
            arrived = (relayed[...] if i == ghost[1] else carry[i]).astype(jnp.float32)
        for frame in range(frames):
            state = partial[i, frame]
            if carried:
                state = state + growth[frame] * arrived
            wide_states[i, frame] = spread(state)

    def product(sources, i):
        taps = [source - i + 1 for source in sources]
        return times([wide_states[source] for source in sources], wout, taps)

    def write(i, value):
        for frame in range(frames):
            updated = lat[frame, i].astype(jnp.float32) + jax.nn.gelu(value[frame])
            result[frame, i] = updated.astype(jnp.bfloat16)
        store(i).start()

    def store(i):
        return pltpu.make_async_copy(result.at[:, i], out_hbm.at[:, place(i, strip)], store_sem.at[i])

    def reach(side):
        return times([wide_states[ghost[side]]], wout, [2 * side])

    def wait_wout():
        for tap in range(3):
            load_wout(tap).wait()

    for i in range(strip):
        prepare(i)
    load_table.wait()
    load_index.wait()
    chosen = index_ref[...]
    decays = jnp.zeros(chosen.shape, jnp.float32)
    for level in range(table_ref.shape[0]):
        decays = jnp.where(chosen == level, table_ref[level], decays)
    growth = [decays]
    for _ in range(frames - 1):
        growth.append(growth[-1] * decays)

    for tap in range(3):
        load_win(tap).wait()
    for tap in range(3):
        load_wout(tap).start()

    middle = list(range(1, bottom))
    first, late = middle[0], middle[1:]

    @block
    def _():
        drive(first)

    pl.semaphore_wait(barrier, total)

    @pl.when(jnp.logical_not(has_before))
    def _():
        if positions > 1:
            begin(first)

    @block
    def _():
        offer(0)
        drive(0)

    send(0)

    @block
    def _():
        for i in late:
            drive(i)
        offer(1)
        drive(bottom)

    send(1)

    def start():
        def far():
            absorb(0, [final], [0])
            if positions > 1:
                begin(0)
            absorb(0, [final], [1])
            if positions > 1:
                begin(ghost[0])

        def lead():
            if positions > 1:
                for i in late:
                    begin(i)

            @guard(1)
            def _():
                absorb(1, [final], [0])

            if positions > 1:
                begin(bottom)

            def pass_turn():
                @guard(1)
                def _():
                    pl.semaphore_signal(turn, inc=1, device_id={"rows": near[1]}, device_id_type=MESH)

            @pl.when(has[0])
            def _():
                far()
                if positions > 1:
                    for i in [*middle, bottom, 0]:
                        sent(i)
                    pass_turn()
                    sent(ghost[0])

            @pl.when(jnp.logical_not(has[0]))
            def _():
                if positions > 1:
                    begin(0)
                    for i in [*middle, bottom]:
                        sent(i)
                    pass_turn()
                    sent(0)

        def second():
            if positions > 1:
                for i in late:
                    begin(i)
            absorb(1, [final], [0])
            if positions > 1:
                pl.semaphore_wait(turn, 1)
                begin(bottom)

            @pl.when(has[0])
            def _():
                far()

            if positions > 1:

                @pl.when(jnp.logical_not(has[0]))
                def _():
                    begin(0)

        @pl.when(odd == 0)
        def _():
            lead()

        @pl.when(odd == 1)
        def _():
            second()

        @guard(1)
        def _():
            absorb(1, [final], [1])
            absorb(1, range(final))

        wait_wout()

        @block
        def _():
            for i in range(1, strip):
                stretch(i, False)
            for i in range(2, bottom):
                write(i, product([i - 1, i, i + 1], i))
            if paired:
                stretch(ghost[1], False)
                write(bottom, product([bottom - 1, bottom], bottom) + reach(1))
            else:
                mixed[bottom] = product([bottom - 1, bottom], bottom)

        if not paired:

            @pl.when(has[1])
            def _():
                stretch(ghost[1], False)
                mixed[bottom] = mixed[bottom] + reach(1)

            write(bottom, mixed[bottom])

        @pl.when(has[0])
        def _():
            absorb(0, range(final))

        @block
        def _():
            stretch(0, False)
            write(1, product([0, 1, 2], 1))
            mixed[0] = product([0, 1], 0)

        @pl.when(has[0])
        def _():
            stretch(ghost[0], False)
            mixed[0] = mixed[0] + reach(0)

        write(0, mixed[0])

    def follow(last):
        def receive(i, pieces=range(PIECES)):
            for piece in pieces:
                advance(i, piece, last)

        def receive_ghost():
            @pl.when(has[0])
            def _():
                absorb(0, [final], [1])
                receive(ghost[0])

        def first_rows():
            stretch(first, True)
            for i in range(first + 2):
                mixed[i] = product([first], i)

        def late_rows():
            for i in late:
                stretch(i, True)
                mixed[i + 1] = product([i], i + 1)
                mixed[i - 1] = mixed[i - 1] + product([i], i - 1)
                mixed[i] = mixed[i] + product([i], i)

        def bottom_rows():
            stretch(bottom, True)
            mixed[bottom] = mixed[bottom] + product([bottom], bottom)
            mixed[bottom - 1] = mixed[bottom - 1] + product([bottom], bottom - 1)
            for i in range(2, bottom):
                write(i, mixed[i])

        def far_rest():
            @pl.when(has[0])
            def _():
                absorb(0, range(final))

        def top_rows():
            stretch(0, True)
            mixed[0] = mixed[0] + product([0], 0)
            write(1, mixed[1] + product([0], 1))

        def core_rows():
            if paired:
                relay_copy().wait_recv()

                @block
                def _():
                    stretch(ghost[1], True)
                    write(bottom, mixed[bottom] + reach(1))
            else:

                @pl.when(has[1])
                def _():
                    relay_copy().wait_recv()
                    stretch(ghost[1], True)
                    mixed[bottom] = mixed[bottom] + reach(1)

                write(bottom, mixed[bottom])

        def early(act):
            (block if last else pl.when(odd == 1))(act)

        def later(act):
            if not last:
                pl.when(odd == 0)(act)

        wait_wout()
        receive(first)
        if last:
            block(first_rows)
        for i in late:
            receive(i)
        if not last:
            early(first_rows)
        early(late_rows)

        @guard(1)
        def _():
            absorb(1, reversed(range(frames)))

        receive(bottom)

        @guard(1)
        def _():
            relay_copy().start()

        if last:
            block(bottom_rows)
            pl.when(odd == 1)(core_rows)

        @pl.when(has[0])
        def _():
            absorb(0, [final], [0])

        receive(0)
        if last:
            far_rest()
            block(top_rows)
            pl.when(odd == 0)(core_rows)
            receive_ghost()
        else:
            receive_ghost()
            later(first_rows)
            later(late_rows)
            block(bottom_rows)
            core_rows()
            far_rest()
            block(top_rows)

        @pl.when(has[0])
        def _():
            stretch(ghost[0], True)
            write(0, mixed[0] + reach(0))

        @pl.when(jnp.logical_not(has[0]))
        def _():
            write(0, mixed[0])

    @pl.when(jnp.logical_not(has_before))
    def _():
        start()

    @pl.when(jnp.logical_and(has_before, has_after))
    def _():
        follow(False)

    @pl.when(jnp.logical_and(has_before, jnp.logical_not(has_after)))
    def _():
        follow(True)

    for side in range(2):

        @pl.when(has[side])
        def _():
            for kind in range(2):
                for frame in range(frames):
                    share_copy(side, kind, frame).wait_send()

    @pl.when(jnp.logical_and(has[1], has_before))
    def _():
        relay_copy().wait_send()

    pending = jnp.logical_and(has_after, jnp.logical_or(has_before, odd == 1))

    @pl.when(pending)
    def _():
        for i in range(strip):
            sent(i)

    @pl.when(jnp.logical_and(has[0], pending))
    def _():
        sent(ghost[0])

    for i in range(strip):
        store(i).wait()


def local(positions, strips, latents, weight_in, weight_out, decay_table, decay_index):
    frames, strip, width, channels = latents.shape
    link = jnp.bfloat16 if positions <= 8 else jnp.float32
    half = jnp.bfloat16
    dma = pltpu.SemaphoreType.DMA
    anywhere = pl.BlockSpec(memory_space=pl.ANY)
    return pl.pallas_call(
        functools.partial(kernel, positions, strips),
        out_shape=jax.ShapeDtypeStruct(latents.shape, latents.dtype),
        in_specs=[anywhere] * 5,
        out_specs=anywhere,
        scratch_shapes=[
            pltpu.VMEM((frames, strip, width, channels), half),
            pltpu.VMEM((9 * channels, channels), half),
            pltpu.VMEM((9 * channels, channels), half),
            pltpu.VMEM((strip, frames, width, 3 * channels), half),
            pltpu.VMEM((strip + 2, frames, width, channels), jnp.float32),
            pltpu.VMEM((2, 2, frames, width, channels), half),
            pltpu.VMEM((2, 2, frames, width, channels), half),
            pltpu.VMEM((strip + 1, width, channels), link),
            pltpu.VMEM((strip + 1, width, channels), link),
            pltpu.VMEM((width, channels), link),
            pltpu.VMEM((strip, frames, width, channels), jnp.float32),
            pltpu.SMEM(decay_table.shape, jnp.float32),
            pltpu.VMEM((1, channels), jnp.int32),
            pltpu.VMEM((strip + 2, frames, width, 3 * channels), half),
            pltpu.VMEM((frames, strip, width, channels), half),
            dma((strip,)),
            dma((3,)),
            dma((3,)),
            dma((2,)),
            dma((strip,)),
            dma((2, 2, frames)),
            dma((2, 2, frames)),
            dma((strip + 1, PIECES)),
            dma((strip + 1, PIECES)),
            dma,
            dma,
            pltpu.SemaphoreType.REGULAR,
        ],
        compiler_params=pltpu.CompilerParams(collective_id=0, has_side_effects=True, vmem_limit_bytes=32 * 1024 * 1024),
    )(
        pltpu.with_memory_space_constraint(latents, pltpu.HBM),
        pltpu.with_memory_space_constraint(weight_in.reshape(3, 3 * channels, channels), pltpu.HBM),
        pltpu.with_memory_space_constraint(weight_out.reshape(3, 3 * channels, channels), pltpu.HBM),
        pltpu.with_memory_space_constraint(decay_table, pltpu.HBM),
        pltpu.with_memory_space_constraint(decay_index.reshape(1, channels), pltpu.HBM),
    )


def solution(mesh):
    in_specs = (P(("groups", "tm"), "rows", None, None), P(), P(), P(), P())
    out_specs = P(("groups", "tm"), "rows", None, None)
    body = functools.partial(local, mesh.shape["tm"], mesh.shape["rows"])
    return jax.shard_map(body, mesh=mesh, in_specs=in_specs, out_specs=out_specs, check_vma=False)
```

time: 18.3 us -> 16.4 us (0.90)
  the two profiles are of different devices: /device:TPU:29 before, /device:TPU:31 now
where the time goes in v1:
time: 16.4 us; the launch traced here: 16.3 us
  Pallas kernels  15.5 us (95%)
  local copies, waits for them, and re-layouts  0.8 us (5%)
    pallas_call x1, Pallas kernels, local(): pl.pallas_call(functools.partial(kernel, positions, strips), out_shape=ja...  15.5 us
    unnamed x1, local copies, waits for them, and re-layouts  0.8 us

profile of v1, /device:TPU:31, one launch (start us, length us, event | category | flops | bytes accessed | tf_op | source)
XLA Modules:
  0.0 16.3 jit_solution(8541422477377414039)
XLA Ops:
  0.0 15.5 %shard_map.55 = bf16[2,4,128,256]{3,2,1,0:T(8,128)(2,1)S(1)} custom-call(bf16[2,4,128,256]{3,2,1,0:T(8,128)(2,1)} %lat_hbm.1, bf16[3,768,256]{2,1,0:T(8,128)(2,1)} %bitcast.3, bf16[3,768,256]{2,1,0:T(8,128)(2,1)} %bitcast.4, f32[16]{0:T(128)} %table_hbm.1, s32[1,256]{1,0:T(1,128)} %bitcast.5), custom_call_target="tpu_custom_call" | custom-call | tf_op jit(solution)/shard_map/pallas_call | solution.py:569
  15.5 0.8 %copy.7 = bf16[2,4,128,256]{3,2,1,0:T(8,128)(2,1)} copy(bf16[2,4,128,256]{3,2,1,0:T(8,128)(2,1)S(1)} %shard_map.55) | data formatting | bytes 1048576

commit v2 on v1

--- a/solution.py
+++ b/solution.py
@@ -1,4 +1,5 @@
 import functools
+import math
 
 import jax
 import jax.numpy as jnp
@@ -9,6 +10,8 @@
 
 MESH = pl.DeviceIdType.MESH
 PIECES = 4
+ROOT = (2.0 / math.pi) ** 0.5
+CUBIC = 0.044715 * ROOT
 
 
 def kernel(
@@ -71,6 +74,22 @@
     def place(i, count):
         return i + odd * (count - 1 - 2 * i)
 
+    def load_lat(i):
+        return pltpu.make_async_copy(lat_hbm.at[:, place(i, strip)], lat.at[:, i], lat_sem.at[i])
+
+    def load_win(tap):
+        return pltpu.make_async_copy(win_hbm.at[place(tap, 3)], win.at[pl.ds(tap * depth, depth)], win_sem.at[tap])
+
+    def load_wout(tap):
+        return pltpu.make_async_copy(wout_hbm.at[place(tap, 3)], wout.at[tap], wout_sem)
+
+    load_table = pltpu.make_async_copy(table_hbm, table_ref, small_sem.at[0])
+    load_index = pltpu.make_async_copy(index_hbm, index_ref, small_sem.at[1])
+
+    for i in range(3):
+        load_lat(i).start()
+    load_win(0).start()
+
     barrier = pltpu.get_barrier_semaphore()
     greeted = (
         (has[0], {"rows": near[0]}),
@@ -86,31 +105,19 @@
         def _():
             pl.semaphore_signal(barrier, inc=1, device_id=where, device_id_type=MESH)
 
-    def load_lat(i):
-        return pltpu.make_async_copy(lat_hbm.at[:, place(i, strip)], lat.at[:, i], lat_sem.at[i])
-
-    def load_win(tap):
-        return pltpu.make_async_copy(win_hbm.at[place(tap, 3)], win.at[pl.ds(tap * depth, depth)], win_sem.at[tap])
-
-    def load_wout(tap):
-        return pltpu.make_async_copy(wout_hbm.at[place(tap, 3)], wout.at[pl.ds(tap * depth, depth)], wout_sem.at[tap])
-
-    load_table = pltpu.make_async_copy(table_hbm, table_ref, small_sem.at[0])
-    load_index = pltpu.make_async_copy(index_hbm, index_ref, small_sem.at[1])
-
     load_table.start()
     load_index.start()
-    for i in range(strip):
+    for tap in range(1, 3):
+        load_win(tap).start()
+    for i in range(3, strip):
         load_lat(i).start()
-    for tap in range(3):
-        load_win(tap).start()
 
     def share_copy(side, kind, frame):
         return pltpu.make_async_remote_copy(
-            src_ref=share.at[side, kind, frame],
-            dst_ref=shared.at[side, kind, frame],
-            send_sem=share_send.at[side, kind, frame],
-            recv_sem=share_recv.at[side, kind, frame],
+            src_ref=share.at[side, frame, kind],
+            dst_ref=shared.at[side, frame, kind],
+            send_sem=share_send.at[side],
+            recv_sem=share_recv.at[side, kind if frame == final else 2],
             device_id={"rows": near[side]},
             device_id_type=MESH,
         )
@@ -130,7 +137,7 @@
         return pltpu.make_async_remote_copy(
             src_ref=passed.at[i, part],
             dst_ref=carry.at[i, part],
-            send_sem=carry_send.at[i, piece],
+            send_sem=carry_send.at[min(i, 1) if i < strip else 2],
             recv_sem=carry_recv.at[i, piece],
             device_id={"tm": moment + 1},
             device_id_type=MESH,
@@ -146,14 +153,16 @@
         return jnp.concatenate([before.astype(jnp.bfloat16), middle, after.astype(jnp.bfloat16)], axis=-1)
 
     def prepare(i):
-        load_lat(i).wait()
         for frame in range(frames):
             wide[i, frame] = spread(lat[frame, i])
 
     def times(rows, weights, taps):
         window = [r.reshape(frames * width, 3 * channels) for r in rows]
         window = window[0] if len(rows) == 1 else jnp.concatenate(window, axis=-1)
-        factor = weights[taps[0] * depth : (taps[-1] + 1) * depth]
+        if len(weights.shape) == 3:
+            factor = weights[taps[0] : taps[-1] + 1].reshape(len(taps) * depth, channels)
+        else:
+            factor = weights[taps[0] * depth : (taps[-1] + 1) * depth]
         value = jnp.dot(window, factor, preferred_element_type=jnp.float32)
         return value.reshape(frames, width, channels)
 
@@ -169,13 +178,13 @@
         for frame in range(frames):
             partial[i, frame] = states[frame]
             if i in edge:
-                share[edge.index(i), 1, frame] = states[frame].astype(jnp.bfloat16)
+                share[edge.index(i), frame, 1] = states[frame].astype(jnp.bfloat16)
 
     def offer(side):
         states = scan(times([wide[edge[side]]], win, [2 - 2 * side]))
         for frame in range(frames):
             partial[ghost[side], frame] = states[frame]
-            share[side, 0, frame] = states[frame].astype(jnp.bfloat16)
+            share[side, frame, 0] = states[frame].astype(jnp.bfloat16)
 
     def send(side):
         @guard(side)
@@ -184,12 +193,39 @@
                 for kind in range(2):
                     share_copy(side, kind, frame).start()
 
-    def absorb(side, which, kinds=(0, 1)):
-        for frame in which:
-            for kind in kinds:
-                share_copy(side, kind, frame).wait_recv()
-                i = (edge, ghost)[kind][side]
-                partial[i, frame] = partial[i, frame] + shared[side, kind, frame].astype(jnp.float32)
+    def add_share(side, kind, frame):
+        i = (edge, ghost)[kind][side]
+        partial[i, frame] = partial[i, frame] + shared[side, frame, kind].astype(jnp.float32)
+
+    def absorb(side, kind):
+        share_copy(side, kind, final).wait_recv()
+        add_share(side, kind, final)
+
+    def absorb_rest(side):
+        if final == 0:
+            return
+        part = pl.ds(0, final)
+        pltpu.make_async_remote_copy(
+            src_ref=share.at[side, part],
+            dst_ref=shared.at[side, part],
+            send_sem=share_send.at[side],
+            recv_sem=share_recv.at[side, 2],
+            device_id={"rows": near[side]},
+            device_id_type=MESH,
+        ).wait_recv()
+        for frame in range(final):
+            for kind in range(2):
+                add_share(side, kind, frame)
+
+    def share_sent(side):
+        pltpu.make_async_remote_copy(
+            src_ref=share.at[side],
+            dst_ref=shared.at[side],
+            send_sem=share_send.at[side],
+            recv_sem=share_recv.at[side, 2],
+            device_id={"rows": near[side]},
+            device_id_type=MESH,
+        ).wait_send()
 
     def block(act):
         pl.when(row >= 0)(act)
@@ -208,9 +244,16 @@
             passed[i, part] = value.astype(passed.dtype)
             carry_copy(i, piece).start()
 
-    def sent(i, pieces=range(PIECES)):
-        for piece in pieces:
-            carry_copy(i, piece).wait_send()
+    def sent(group):
+        part = (pl.ds(0, 1), pl.ds(1, strip - 1), pl.ds(strip, 1))[group]
+        pltpu.make_async_remote_copy(
+            src_ref=passed.at[part],
+            dst_ref=carry.at[part],
+            send_sem=carry_send.at[(0, 1, 2)[group]],
+            recv_sem=carry_recv.at[0, 0],
+            device_id={"tm": moment + 1},
+            device_id_type=MESH,
+        ).wait_send()
 
     def stretch(i, carried):
         if carried:
@@ -227,21 +270,26 @@
 
     def write(i, value):
         for frame in range(frames):
-            updated = lat[frame, i].astype(jnp.float32) + jax.nn.gelu(value[frame])
+            x = value[frame]
+            half = 0.5 * x
+            angle = x * (ROOT + CUBIC * (x * x))
+            updated = lat[frame, i].astype(jnp.float32) + (half + half * jnp.tanh(angle))
             result[frame, i] = updated.astype(jnp.bfloat16)
         store(i).start()
 
     def store(i):
-        return pltpu.make_async_copy(result.at[:, i], out_hbm.at[:, place(i, strip)], store_sem.at[i])
+        return pltpu.make_async_copy(result.at[:, i], out_hbm.at[:, place(i, strip)], store_sem)
 
     def reach(side):
         return times([wide_states[ghost[side]]], wout, [2 * side])
 
     def wait_wout():
-        for tap in range(3):
-            load_wout(tap).wait()
-
-    for i in range(strip):
+        pltpu.make_async_copy(wout_hbm, wout, wout_sem).wait()
+
+    middle = list(range(1, bottom))
+    first, late = middle[0], middle[1:]
+    for i in range(3):
+        load_lat(i).wait()
         prepare(i)
     load_table.wait()
     load_index.wait()
@@ -252,48 +300,74 @@
     growth = [decays]
     for _ in range(frames - 1):
         growth.append(growth[-1] * decays)
-
-    for tap in range(3):
-        load_win(tap).wait()
+    load_win(0).wait()
+
+    @block
+    def _():
+        partial[first] = times([wide[0]], win, [0])
+
+    load_win(1).wait()
+    load_win(2).wait()
+
+    @block
+    def _():
+        value = times([wide[1]], win, [1]) + times([wide[2]], win, [2])
+        states = scan(partial[first] + value)
+        for frame in range(frames):
+            partial[first, frame] = states[frame]
+
+    for i in range(3, strip):
+        load_lat(i).wait()
+        prepare(i)
+
+    pl.semaphore_wait(barrier, total)
+
+    leads = jnp.logical_and(jnp.logical_not(has_before), odd == 1)
+
+    @pl.when(leads)
+    def _():
+        if positions > 1:
+            begin(first)
+        for i in late:
+            drive(i)
+            if positions > 1:
+                begin(i)
+
+    @block
+    def _():
+        offer(0)
+        drive(0)
+
+    send(0)
+
+    @pl.when(jnp.logical_and(jnp.logical_not(has_before), odd == 0))
+    def _():
+        if positions > 1:
+            begin(first)
+
     for tap in range(3):
         load_wout(tap).start()
 
-    middle = list(range(1, bottom))
-    first, late = middle[0], middle[1:]
-
-    @block
-    def _():
-        drive(first)
-
-    pl.semaphore_wait(barrier, total)
-
-    @pl.when(jnp.logical_not(has_before))
-    def _():
-        if positions > 1:
-            begin(first)
-
-    @block
-    def _():
-        offer(0)
-        drive(0)
-
-    send(0)
-
-    @block
+    @pl.when(jnp.logical_not(leads))
     def _():
         for i in late:
             drive(i)
         offer(1)
         drive(bottom)
 
+    @pl.when(leads)
+    def _():
+        offer(1)
+        drive(bottom)
+
     send(1)
 
     def start():
         def far():
-            absorb(0, [final], [0])
+            absorb(0, 0)
             if positions > 1:
                 begin(0)
-            absorb(0, [final], [1])
+            absorb(0, 1)
             if positions > 1:
                 begin(ghost[0])
 
@@ -304,7 +378,7 @@
 
             @guard(1)
             def _():
-                absorb(1, [final], [0])
+                absorb(1, 0)
 
             if positions > 1:
                 begin(bottom)
@@ -318,28 +392,24 @@
             def _():
                 far()
                 if positions > 1:
-                    for i in [*middle, bottom, 0]:
-                        sent(i)
+                    sent(1)
+                    sent(0)
                     pass_turn()
-                    sent(ghost[0])
+                    sent(2)
 
             @pl.when(jnp.logical_not(has[0]))
             def _():
                 if positions > 1:
                     begin(0)
-                    for i in [*middle, bottom]:
-                        sent(i)
+                    sent(1)
                     pass_turn()
                     sent(0)
 
         def second():
+            absorb(1, 0)
             if positions > 1:
-                for i in late:
-                    begin(i)
-            absorb(1, [final], [0])
-            if positions > 1:
+                begin(bottom)
                 pl.semaphore_wait(turn, 1)
-                begin(bottom)
 
             @pl.when(has[0])
             def _():
@@ -361,8 +431,8 @@
 
         @guard(1)
         def _():
-            absorb(1, [final], [1])
-            absorb(1, range(final))
+            absorb(1, 1)
+            absorb_rest(1)
 
         wait_wout()
 
@@ -389,7 +459,7 @@
 
         @pl.when(has[0])
         def _():
-            absorb(0, range(final))
+            absorb_rest(0)
 
         @block
         def _():
@@ -412,7 +482,7 @@
         def receive_ghost():
             @pl.when(has[0])
             def _():
-                absorb(0, [final], [1])
+                absorb(0, 1)
                 receive(ghost[0])
 
         def first_rows():
@@ -427,17 +497,19 @@
                 mixed[i - 1] = mixed[i - 1] + product([i], i - 1)
                 mixed[i] = mixed[i] + product([i], i)
 
-        def bottom_rows():
+        def bottom_rows(done=False):
             stretch(bottom, True)
             mixed[bottom] = mixed[bottom] + product([bottom], bottom)
             mixed[bottom - 1] = mixed[bottom - 1] + product([bottom], bottom - 1)
             for i in range(2, bottom):
                 write(i, mixed[i])
+            if done:
+                write(bottom, mixed[bottom])
 
         def far_rest():
             @pl.when(has[0])
             def _():
-                absorb(0, range(final))
+                absorb_rest(0)
 
         def top_rows():
             stretch(0, True)
@@ -445,22 +517,35 @@
             write(1, mixed[1] + product([0], 1))
 
         def core_rows():
-            if paired:
+            @guard(1)
+            def _():
                 relay_copy().wait_recv()
 
                 @block
                 def _():
                     stretch(ghost[1], True)
-                    write(bottom, mixed[bottom] + reach(1))
+                    mixed[bottom] = mixed[bottom] + reach(1)
+
+        waits = jnp.logical_and(has[0], odd == 1)
+
+        def core_close():
+            if paired:
+                relay_copy().wait_recv()
+                stretch(ghost[1], True)
+                write(bottom, mixed[bottom] + reach(1))
             else:
-
-                @pl.when(has[1])
-                def _():
-                    relay_copy().wait_recv()
-                    stretch(ghost[1], True)
-                    mixed[bottom] = mixed[bottom] + reach(1)
-
+                core_rows()
                 write(bottom, mixed[bottom])
+
+        def ghost_rows():
+            @pl.when(has[0])
+            def _():
+                stretch(ghost[0], True)
+                write(0, mixed[0] + reach(0))
+
+            @pl.when(jnp.logical_not(has[0]))
+            def _():
+                write(0, mixed[0])
 
         def early(act):
             (block if last else pl.when(odd == 1))(act)
@@ -481,7 +566,9 @@
 
         @guard(1)
         def _():
-            absorb(1, reversed(range(frames)))
+            absorb(1, 0)
+            absorb(1, 1)
+            absorb_rest(1)
 
         receive(bottom)
 
@@ -490,36 +577,31 @@
             relay_copy().start()
 
         if last:
+
             block(bottom_rows)
-            pl.when(odd == 1)(core_rows)
+
+            pl.when(jnp.logical_not(waits))(core_close)
 
         @pl.when(has[0])
         def _():
-            absorb(0, [final], [0])
+            absorb(0, 0)
 
         receive(0)
         if last:
             far_rest()
             block(top_rows)
-            pl.when(odd == 0)(core_rows)
+            pl.when(waits)(core_close)
             receive_ghost()
+            ghost_rows()
         else:
             receive_ghost()
             later(first_rows)
             later(late_rows)
-            block(bottom_rows)
             core_rows()
+            block(lambda: bottom_rows(True))
             far_rest()
             block(top_rows)
-
-        @pl.when(has[0])
-        def _():
-            stretch(ghost[0], True)
-            write(0, mixed[0] + reach(0))
-
-        @pl.when(jnp.logical_not(has[0]))
-        def _():
-            write(0, mixed[0])
+            ghost_rows()
 
     @pl.when(jnp.logical_not(has_before))
     def _():
@@ -537,9 +619,7 @@
 
         @pl.when(has[side])
         def _():
-            for kind in range(2):
-                for frame in range(frames):
-                    share_copy(side, kind, frame).wait_send()
+            share_sent(side)
 
     @pl.when(jnp.logical_and(has[1], has_before))
     def _():
@@ -549,15 +629,14 @@
 
     @pl.when(pending)
     def _():
-        for i in range(strip):
-            sent(i)
+        sent(1)
+        sent(0)
 
     @pl.when(jnp.logical_and(has[0], pending))
     def _():
-        sent(ghost[0])
-
-    for i in range(strip):
-        store(i).wait()
+        sent(2)
+
+    pltpu.make_async_copy(result, out_hbm, store_sem).wait()
 
 
 def local(positions, strips, latents, weight_in, weight_out, decay_table, decay_index):
@@ -574,11 +653,11 @@
         scratch_shapes=[
             pltpu.VMEM((frames, strip, width, channels), half),
             pltpu.VMEM((9 * channels, channels), half),
-            pltpu.VMEM((9 * channels, channels), half),
+            pltpu.VMEM((3, 3 * channels, channels), half),
             pltpu.VMEM((strip, frames, width, 3 * channels), half),
             pltpu.VMEM((strip + 2, frames, width, channels), jnp.float32),
-            pltpu.VMEM((2, 2, frames, width, channels), half),
-            pltpu.VMEM((2, 2, frames, width, channels), half),
+            pltpu.VMEM((2, frames, 2, width, channels), half),
+            pltpu.VMEM((2, frames, 2, width, channels), half),
             pltpu.VMEM((strip + 1, width, channels), link),
             pltpu.VMEM((strip + 1, width, channels), link),
             pltpu.VMEM((width, channels), link),
@@ -589,12 +668,12 @@
             pltpu.VMEM((frames, strip, width, channels), half),
             dma((strip,)),
             dma((3,)),
+            dma,
+            dma((2,)),
+            dma,
+            dma((2,)),
+            dma((2, 3)),
             dma((3,)),
-            dma((2,)),
-            dma((strip,)),
-            dma((2, 2, frames)),
-            dma((2, 2, frames)),
-            dma((strip + 1, PIECES)),
             dma((strip + 1, PIECES)),
             dma,
             dma,

time: 16.4 us -> 15.8 us (0.963)
  the two profiles are of different devices: /device:TPU:31 before, /device:TPU:29 now
where the time goes in v2:
time: 15.8 us; the launch traced here: 15.6 us
  Pallas kernels  14.8 us (94%)
  local copies, waits for them, and re-layouts  0.8 us (5%)
    pallas_call x1, Pallas kernels, local(): pl.pallas_call(functools.partial(kernel, positions, strips), out_shape=ja...  14.8 us
    unnamed x1, local copies, waits for them, and re-layouts  0.8 us

profile of v2, /device:TPU:29, one launch (start us, length us, event | category | flops | bytes accessed | tf_op | source)
XLA Modules:
  0.0 15.6 jit_solution(16736608032505383952)
XLA Ops:
  0.0 14.8 %shard_map.55 = bf16[2,4,128,256]{3,2,1,0:T(8,128)(2,1)S(1)} custom-call(bf16[2,4,128,256]{3,2,1,0:T(8,128)(2,1)} %lat_hbm.1, bf16[3,768,256]{2,1,0:T(8,128)(2,1)} %bitcast.3, bf16[3,768,256]{2,1,0:T(8,128)(2,1)} %bitcast.4, f32[16]{0:T(128)} %table_hbm.1, s32[1,256]{1,0:T(1,128)} %bitcast.5), custom_call_target="tpu_custom_call" | custom-call | tf_op jit(solution)/shard_map/pallas_call | solution.py:648
  14.8 0.8 %copy.7 = bf16[2,4,128,256]{3,2,1,0:T(8,128)(2,1)} copy(bf16[2,4,128,256]{3,2,1,0:T(8,128)(2,1)S(1)} %shard_map.55) | data formatting | bytes 1048576

commit v3 on v2

--- a/solution.py
+++ b/solution.py
@@ -22,7 +22,7 @@
     wout_hbm,
     table_hbm,
     index_hbm,
-    out_hbm,
+    out,
     lat,
     win,
     wout,
@@ -37,12 +37,10 @@
     table_ref,
     index_ref,
     wide_states,
-    result,
     lat_sem,
     win_sem,
     wout_sem,
     small_sem,
-    store_sem,
     share_send,
     share_recv,
     carry_send,
@@ -75,7 +73,7 @@
         return i + odd * (count - 1 - 2 * i)
 
     def load_lat(i):
-        return pltpu.make_async_copy(lat_hbm.at[:, place(i, strip)], lat.at[:, i], lat_sem.at[i])
+        return pltpu.make_async_copy(lat_hbm.at[:, place(i, strip)], lat.at[:, i], lat_sem.at[0 if i < 3 else 1])
 
     def load_win(tap):
         return pltpu.make_async_copy(win_hbm.at[place(tap, 3)], win.at[pl.ds(tap * depth, depth)], win_sem.at[tap])
@@ -268,17 +266,42 @@
         taps = [source - i + 1 for source in sources]
         return times([wide_states[source] for source in sources], wout, taps)
 
+    def update(base, x):
+        half = 0.5 * x
+        angle = x * (ROOT + CUBIC * (x * x))
+        return (base.astype(jnp.float32) + (half + half * jnp.tanh(angle))).astype(jnp.bfloat16)
+
     def write(i, value):
         for frame in range(frames):
-            x = value[frame]
-            half = 0.5 * x
-            angle = x * (ROOT + CUBIC * (x * x))
-            updated = lat[frame, i].astype(jnp.float32) + (half + half * jnp.tanh(angle))
-            result[frame, i] = updated.astype(jnp.bfloat16)
-        store(i).start()
-
-    def store(i):
-        return pltpu.make_async_copy(result.at[:, i], out_hbm.at[:, place(i, strip)], store_sem)
+            out[frame, place(i, strip)] = update(lat[frame, i], value[frame])
+
+    cut = width // 2
+
+    def stretch_half(i, half):
+        low, count = (0, cut + span) if half == 0 else (cut - span, cut + span)
+        part = pl.ds(low, count)
+        keep = slice(0, cut) if half == 0 else slice(span, span + cut)
+        place_of = lax.broadcasted_iota(jnp.int32, (count, channels), 0)
+        arrived = carry[i, part].astype(jnp.float32)
+        for frame in range(frames):
+            full = partial[i, frame, part] + growth[frame] * arrived
+            before, after = pltpu.roll(full, 1, 0), pltpu.roll(full, count - 1, 0)
+            if half == 0:
+                before = jnp.where(place_of == 0, 0.0, before)
+            else:
+                after = jnp.where(place_of == count - 1, 0.0, after)
+            whole = jnp.concatenate([v.astype(jnp.bfloat16) for v in (before, full, after)], axis=-1)
+            wide_states[i, frame, pl.ds(half * cut, cut)] = whole[keep]
+
+    def half_times(i, half, tap):
+        window = wide_states[i, :, pl.ds(half * cut, cut)].reshape(frames * cut, 3 * channels)
+        value = jnp.dot(window, wout[tap], preferred_element_type=jnp.float32)
+        return value.reshape(frames, cut, channels)
+
+    def write_half(i, half, value):
+        part = pl.ds(half * cut, cut)
+        for frame in range(frames):
+            out[frame, place(i, strip), part] = update(lat[frame, i, part], value[frame])
 
     def reach(side):
         return times([wide_states[ghost[side]]], wout, [2 * side])
@@ -288,8 +311,9 @@
 
     middle = list(range(1, bottom))
     first, late = middle[0], middle[1:]
+    rows = pl.ds(0, 3)
+    pltpu.make_async_copy(lat_hbm.at[:, rows], lat.at[:, rows], lat_sem.at[0]).wait()
     for i in range(3):
-        load_lat(i).wait()
         prepare(i)
     load_table.wait()
     load_index.wait()
@@ -316,8 +340,9 @@
         for frame in range(frames):
             partial[first, frame] = states[frame]
 
+    rows = pl.ds(3, strip - 3)
+    pltpu.make_async_copy(lat_hbm.at[:, rows], lat.at[:, rows], lat_sem.at[1]).wait()
     for i in range(3, strip):
-        load_lat(i).wait()
         prepare(i)
 
     pl.semaphore_wait(barrier, total)
@@ -582,18 +607,47 @@
 
             pl.when(jnp.logical_not(waits))(core_close)
 
-        @pl.when(has[0])
-        def _():
+        early_pieces, last_piece = range(PIECES - 1), [PIECES - 1]
+
+        def top_half(half):
+            part = pl.ds(half * cut, cut)
+            stretch_half(0, half)
+            one = mixed[1, :, part] + half_times(0, half, 0)
+            two = mixed[0, :, part] + half_times(0, half, 1)
+            write_half(1, half, one)
+            write_half(0, half, two)
+
+        def free_end():
+            receive(0, early_pieces)
+            top_half(0)
+            receive(0, last_piece)
+            top_half(1)
+
+        def far_end():
             absorb(0, 0)
-
-        receive(0)
+            receive(0)
+            absorb_rest(0)
+            block(top_rows)
+
+            pl.when(odd == 1)(core_close)
+            absorb(0, 1)
+            receive(ghost[0])
+
+            @block
+            def _():
+                stretch(ghost[0], True)
+                write(0, mixed[0] + reach(0))
+
         if last:
-            far_rest()
-            block(top_rows)
-            pl.when(waits)(core_close)
-            receive_ghost()
-            ghost_rows()
+            pl.when(jnp.logical_not(has[0]))(free_end)
+            pl.when(has[0])(far_end)
         else:
+
+            @pl.when(has[0])
+            def _():
+                absorb(0, 0)
+
+            receive(0)
             receive_ghost()
             later(first_rows)
             later(late_rows)
@@ -635,8 +689,6 @@
     @pl.when(jnp.logical_and(has[0], pending))
     def _():
         sent(2)
-
-    pltpu.make_async_copy(result, out_hbm, store_sem).wait()
 
 
 def local(positions, strips, latents, weight_in, weight_out, decay_table, decay_index):
@@ -649,7 +701,7 @@
         functools.partial(kernel, positions, strips),
         out_shape=jax.ShapeDtypeStruct(latents.shape, latents.dtype),
         in_specs=[anywhere] * 5,
-        out_specs=anywhere,
+        out_specs=pl.BlockSpec(memory_space=pltpu.VMEM),
         scratch_shapes=[
             pltpu.VMEM((frames, strip, width, channels), half),
             pltpu.VMEM((9 * channels, channels), half),
@@ -665,12 +717,10 @@
             pltpu.SMEM(decay_table.shape, jnp.float32),
             pltpu.VMEM((1, channels), jnp.int32),
             pltpu.VMEM((strip + 2, frames, width, 3 * channels), half),
-            pltpu.VMEM((frames, strip, width, channels), half),
-            dma((strip,)),
+            dma((2,)),
             dma((3,)),
             dma,
             dma((2,)),
-            dma,
             dma((2,)),
             dma((2, 3)),
             dma((3,)),

time: 15.8 us -> 15.5 us (0.981)
  Pallas kernels: 14.8 us -> 14.5 us
    pallas_call x1, Pallas kernels: 14.8 us -> 14.5 us  [local(): pl.pallas_call(functools.partial(kernel, positions, strips), out_shape=ja...]
where the time goes in v3:
time: 15.5 us; the launch traced here: 15.3 us
  Pallas kernels  14.5 us (94%)
  local copies, waits for them, and re-layouts  0.8 us (5%)
    pallas_call x1, Pallas kernels, local(): pl.pallas_call(functools.partial(kernel, positions, strips), out_shape=ja...  14.5 us
    unnamed x1, local copies, waits for them, and re-layouts  0.8 us

profile of v3, /device:TPU:29, one launch (start us, length us, event | category | flops | bytes accessed | tf_op | source)
XLA Modules:
  0.0 15.3 jit_solution(14580832072678184282)
XLA Ops:
  0.0 14.5 %shard_map.55 = bf16[2,4,128,256]{3,2,1,0:T(8,128)(2,1)S(1)} custom-call(bf16[2,4,128,256]{3,2,1,0:T(8,128)(2,1)} %lat_hbm.1, bf16[3,768,256]{2,1,0:T(8,128)(2,1)} %bitcast.3, bf16[3,768,256]{2,1,0:T(8,128)(2,1)} %bitcast.4, f32[16]{0:T(128)} %table_hbm.1, s32[1,256]{1,0:T(1,128)} %bitcast.5), custom_call_target="tpu_custom_call" | custom-call | tf_op jit(solution)/shard_map/pallas_call | solution.py:700
  14.5 0.8 %copy.7 = bf16[2,4,128,256]{3,2,1,0:T(8,128)(2,1)} copy(bf16[2,4,128,256]{3,2,1,0:T(8,128)(2,1)S(1)} %shard_map.55) | data formatting | bytes 1048576

commit v4 on v3

--- a/solution.py
+++ b/solution.py
@@ -12,6 +12,12 @@
 PIECES = 4
 ROOT = (2.0 / math.pi) ** 0.5
 CUBIC = 0.044715 * ROOT
+
+
+def update(base, x):
+    half = 0.5 * x
+    angle = x * (ROOT + CUBIC * (x * x))
+    return (base.astype(jnp.float32) + (half + half * jnp.tanh(angle))).astype(jnp.bfloat16)
 
 
 def kernel(
@@ -23,6 +29,8 @@
     table_hbm,
     index_hbm,
     out,
+    kept,
+    open_row,
     lat,
     win,
     wout,
@@ -266,13 +274,11 @@
         taps = [source - i + 1 for source in sources]
         return times([wide_states[source] for source in sources], wout, taps)
 
-    def update(base, x):
-        half = 0.5 * x
-        angle = x * (ROOT + CUBIC * (x * x))
-        return (base.astype(jnp.float32) + (half + half * jnp.tanh(angle))).astype(jnp.bfloat16)
-
     def write(i, value):
         for frame in range(frames):
+            if i == 0:
+                open_row[frame] = value[frame]
+                continue
             out[frame, place(i, strip)] = update(lat[frame, i], value[frame])
 
     cut = width // 2
@@ -301,6 +307,9 @@
     def write_half(i, half, value):
         part = pl.ds(half * cut, cut)
         for frame in range(frames):
+            if i == 0:
+                open_row[frame, part] = value[frame]
+                continue
             out[frame, place(i, strip), part] = update(lat[frame, i, part], value[frame])
 
     def reach(side):
@@ -345,6 +354,7 @@
     for i in range(3, strip):
         prepare(i)
 
+    kept[...] = lat[:, 0]
     pl.semaphore_wait(barrier, total)
 
     leads = jnp.logical_and(jnp.logical_not(has_before), odd == 1)
@@ -697,11 +707,15 @@
     half = jnp.bfloat16
     dma = pltpu.SemaphoreType.DMA
     anywhere = pl.BlockSpec(memory_space=pl.ANY)
-    return pl.pallas_call(
+    done = pl.pallas_call(
         functools.partial(kernel, positions, strips),
-        out_shape=jax.ShapeDtypeStruct(latents.shape, latents.dtype),
+        out_shape=[
+            jax.ShapeDtypeStruct(latents.shape, latents.dtype),
+            jax.ShapeDtypeStruct((frames, width, channels), latents.dtype),
+            jax.ShapeDtypeStruct((frames, width, channels), jnp.float32),
+        ],
         in_specs=[anywhere] * 5,
-        out_specs=pl.BlockSpec(memory_space=pltpu.VMEM),
+        out_specs=[pl.BlockSpec(memory_space=pltpu.VMEM)] * 3,
         scratch_shapes=[
             pltpu.VMEM((frames, strip, width, channels), half),
             pltpu.VMEM((9 * channels, channels), half),
@@ -737,6 +751,27 @@
         pltpu.with_memory_space_constraint(decay_table, pltpu.HBM),
         pltpu.with_memory_space_constraint(decay_index.reshape(1, channels), pltpu.HBM),
     )
+    return pl.pallas_call(
+        hand_out,
+        out_shape=jax.ShapeDtypeStruct(latents.shape, latents.dtype),
+        in_specs=[pl.BlockSpec(memory_space=pl.ANY)] + [pl.BlockSpec(memory_space=pltpu.VMEM)] * 2,
+        out_specs=pl.BlockSpec(memory_space=pltpu.HBM),
+        scratch_shapes=[pltpu.VMEM((frames, width, channels), half), dma((2,))],
+    )(*[pltpu.with_memory_space_constraint(value, pltpu.VMEM) for value in done])
+
+
+def hand_out(source, kept, open_row, target, row_out, sem):
+    frames, strip = source.shape[:2]
+    odd = lax.rem(lax.axis_index("rows"), 2)
+    rest = pl.ds(1 - odd, strip - 1)
+    first = pltpu.make_async_copy(source.at[:, rest], target.at[:, rest], sem.at[0])
+    second = pltpu.make_async_copy(row_out, target.at[:, odd * (strip - 1)], sem.at[1])
+    first.start()
+    for frame in range(frames):
+        row_out[frame] = update(kept[frame], open_row[frame])
+    second.start()
+    first.wait()
+    second.wait()
 
 
 def solution(mesh):

time: 15.5 us -> 15.4 us (level)
  Pallas kernels: 14.5 us -> 15.3 us
  local copies, waits for them, and re-layouts: 0.8 us -> 0 us
    unnamed x1 -> x0, local copies, waits for them, and re-layouts: 0.8 us -> none
    pallas_call x1 -> x2, Pallas kernels: 14.5 us -> 15.3 us  [the longest x1 14.5 us: local(): pl.pallas_call(functools.partial(kernel, positions, strips), out_shape=[j...]
where the time goes in v4:
time: 15.4 us; the launch traced here: 15.3 us
  Pallas kernels  15.3 us (99%)
    pallas_call x1, Pallas kernels, local(): pl.pallas_call(functools.partial(kernel, positions, strips), out_shape=[j...  14.5 us
    pallas_call x1, Pallas kernels, local(): pl.pallas_call(hand_out, out_shape=jax.ShapeDtypeStruct(latents.shape, la...  0.81 us

profile of v4, /device:TPU:29, one launch (start us, length us, event | category | flops | bytes accessed | tf_op | source)
XLA Modules:
  0.0 15.3 jit_solution(17944747762851880974)
XLA Ops:
  0.0 14.5 %shard_map.55 = (bf16[2,4,128,256]{3,2,1,0:T(8,128)(2,1)S(1)}, bf16[2,128,256]{2,1,0:T(8,128)(2,1)S(1)}, f32[2,128,256]{2,1,0:T(8,128)S(1)}) custom-call(bf16[2,4,128,256]{3,2,1,0:T(8,128)(2,1)} %lat_hbm.1, bf16[3,768,256]{2,1,0:T(8,128)(2,1)} %bitcast.3, bf16[3,768,256]{2,1,0:T(8,128)(2,1)} %bitcast.4, f32[16]{0:T(128)} %table_hbm.1, s32[1,256]{1,0:T(1,128)} %bitcast.5), custom_call_target="tpu_custom_call" | custom-call | tf_op jit(solution)/shard_map/pallas_call | solution.py:710
  14.5 0.8 %shard_map.56 = bf16[2,4,128,256]{3,2,1,0:T(8,128)(2,1)} custom-call(bf16[2,4,128,256]{3,2,1,0:T(8,128)(2,1)S(1)} %get-tuple-element.8.source, bf16[2,128,256]{2,1,0:T(8,128)(2,1)S(1)} %get-tuple-element.9.kept, f32[2,128,256]{2,1,0:T(8,128)S(1)} %get-tuple-element.10.open_row), custom_call_target="tpu_custom_call" | custom-call | tf_op jit(solution)/shard_map/pallas_call | solution.py:754

commit v5 on v4

--- a/solution.py
+++ b/solution.py
@@ -756,7 +756,7 @@
         out_shape=jax.ShapeDtypeStruct(latents.shape, latents.dtype),
         in_specs=[pl.BlockSpec(memory_space=pl.ANY)] + [pl.BlockSpec(memory_space=pltpu.VMEM)] * 2,
         out_specs=pl.BlockSpec(memory_space=pltpu.HBM),
-        scratch_shapes=[pltpu.VMEM((frames, width, channels), half), dma((2,))],
+        scratch_shapes=[pltpu.VMEM((frames, width, channels), half), dma((1 + frames,))],
     )(*[pltpu.with_memory_space_constraint(value, pltpu.VMEM) for value in done])
 
 
@@ -765,13 +765,16 @@
     odd = lax.rem(lax.axis_index("rows"), 2)
     rest = pl.ds(1 - odd, strip - 1)
     first = pltpu.make_async_copy(source.at[:, rest], target.at[:, rest], sem.at[0])
-    second = pltpu.make_async_copy(row_out, target.at[:, odd * (strip - 1)], sem.at[1])
     first.start()
+    parts = []
     for frame in range(frames):
         row_out[frame] = update(kept[frame], open_row[frame])
-    second.start()
+        part = pltpu.make_async_copy(row_out.at[frame], target.at[frame, odd * (strip - 1)], sem.at[1 + frame])
+        part.start()
+        parts.append(part)
     first.wait()
-    second.wait()
+    for part in parts:
+        part.wait()
 
 
 def solution(mesh):

time: 15.4 us -> 15.5 us (level)
  no operation moved by 1% of the time
where the time goes in v5:
time: 15.5 us; the launch traced here: 15.3 us
  Pallas kernels  15.3 us (99%)
    pallas_call x1, Pallas kernels, local(): pl.pallas_call(functools.partial(kernel, positions, strips), out_shape=[j...  14.5 us
    pallas_call x1, Pallas kernels, local(): pl.pallas_call(hand_out, out_shape=jax.ShapeDtypeStruct(latents.shape, la...  0.82 us

profile of v5, /device:TPU:29, one launch (start us, length us, event | category | flops | bytes accessed | tf_op | source)
XLA Modules:
  0.0 15.3 jit_solution(2820568772944767344)
XLA Ops:
  0.0 14.5 %shard_map.55 = (bf16[2,4,128,256]{3,2,1,0:T(8,128)(2,1)S(1)}, bf16[2,128,256]{2,1,0:T(8,128)(2,1)S(1)}, f32[2,128,256]{2,1,0:T(8,128)S(1)}) custom-call(bf16[2,4,128,256]{3,2,1,0:T(8,128)(2,1)} %lat_hbm.1, bf16[3,768,256]{2,1,0:T(8,128)(2,1)} %bitcast.3, bf16[3,768,256]{2,1,0:T(8,128)(2,1)} %bitcast.4, f32[16]{0:T(128)} %table_hbm.1, s32[1,256]{1,0:T(1,128)} %bitcast.5), custom_call_target="tpu_custom_call" | custom-call | tf_op jit(solution)/shard_map/pallas_call | solution.py:710
  14.5 0.8 %shard_map.56 = bf16[2,4,128,256]{3,2,1,0:T(8,128)(2,1)} custom-call(bf16[2,4,128,256]{3,2,1,0:T(8,128)(2,1)S(1)} %get-tuple-element.8.source, bf16[2,128,256]{2,1,0:T(8,128)(2,1)S(1)} %get-tuple-element.9.kept, f32[2,128,256]{2,1,0:T(8,128)S(1)} %get-tuple-element.10.open_row), custom_call_target="tpu_custom_call" | custom-call | tf_op jit(solution)/shard_map/pallas_call | solution.py:754

commit v6 on v5

--- a/solution.py
+++ b/solution.py
@@ -47,7 +47,6 @@
     wide_states,
     lat_sem,
     win_sem,
-    wout_sem,
     small_sem,
     share_send,
     share_recv,
@@ -87,7 +86,7 @@
         return pltpu.make_async_copy(win_hbm.at[place(tap, 3)], win.at[pl.ds(tap * depth, depth)], win_sem.at[tap])
 
     def load_wout(tap):
-        return pltpu.make_async_copy(wout_hbm.at[place(tap, 3)], wout.at[tap], wout_sem)
+        return pltpu.make_async_copy(wout_hbm.at[place(tap, 3)], wout.at[tap], win_sem.at[0])
 
     load_table = pltpu.make_async_copy(table_hbm, table_ref, small_sem.at[0])
     load_index = pltpu.make_async_copy(index_hbm, index_ref, small_sem.at[1])
@@ -316,7 +315,7 @@
         return times([wide_states[ghost[side]]], wout, [2 * side])
 
     def wait_wout():
-        pltpu.make_async_copy(wout_hbm, wout, wout_sem).wait()
+        pltpu.make_async_copy(wout_hbm, wout, win_sem.at[0]).wait()
 
     middle = list(range(1, bottom))
     first, late = middle[0], middle[1:]
@@ -733,7 +732,6 @@
             pltpu.VMEM((strip + 2, frames, width, 3 * channels), half),
             dma((2,)),
             dma((3,)),
-            dma,
             dma((2,)),
             dma((2,)),
             dma((2, 3)),

time: 15.5 us -> 15.4 us (level)
  no operation moved by 1% of the time
where the time goes in v6:
time: 15.4 us; the launch traced here: 15.3 us
  Pallas kernels  15.3 us (99%)
    pallas_call x1, Pallas kernels, local(): pl.pallas_call(functools.partial(kernel, positions, strips), out_shape=[j...  14.5 us
    pallas_call x1, Pallas kernels, local(): pl.pallas_call(hand_out, out_shape=jax.ShapeDtypeStruct(latents.shape, la...  0.82 us

profile of v6, /device:TPU:29, one launch (start us, length us, event | category | flops | bytes accessed | tf_op | source)
XLA Modules:
  0.0 15.3 jit_solution(12855673359365277176)
XLA Ops:
  0.0 14.5 %shard_map.55 = (bf16[2,4,128,256]{3,2,1,0:T(8,128)(2,1)S(1)}, bf16[2,128,256]{2,1,0:T(8,128)(2,1)S(1)}, f32[2,128,256]{2,1,0:T(8,128)S(1)}) custom-call(bf16[2,4,128,256]{3,2,1,0:T(8,128)(2,1)} %lat_hbm.1, bf16[3,768,256]{2,1,0:T(8,128)(2,1)} %bitcast.3, bf16[3,768,256]{2,1,0:T(8,128)(2,1)} %bitcast.4, f32[16]{0:T(128)} %table_hbm.1, s32[1,256]{1,0:T(1,128)} %bitcast.5), custom_call_target="tpu_custom_call" | custom-call | tf_op jit(solution)/shard_map/pallas_call | solution.py:709
  14.5 0.8 %shard_map.56 = bf16[2,4,128,256]{3,2,1,0:T(8,128)(2,1)} custom-call(bf16[2,4,128,256]{3,2,1,0:T(8,128)(2,1)S(1)} %get-tuple-element.8.source, bf16[2,128,256]{2,1,0:T(8,128)(2,1)S(1)} %get-tuple-element.9.kept, f32[2,128,256]{2,1,0:T(8,128)S(1)} %get-tuple-element.10.open_row), custom_call_target="tpu_custom_call" | custom-call | tf_op jit(solution)/shard_map/pallas_call | solution.py:752
